TPU v7x, 256 devices: a whole 4x4x8 slice. The times are simulated.
256 devices in a mesh: leaf: 128 (over x, y, z), col: 2 (over core).
Axes of the slice: x: 4, y: 4, z: 8, core: 2. Of those that a mesh axis runs over, the one named last changes fastest.
Arguments:
- coords: float32 [3, 262144], P(None, 'leaf'), may hold values from -6 to 6
- values: float32 [32, 262144], P('col', 'leaf'), may hold values from -6 to 6
- leaf_basis: float32 [1024, 256, 128], P('leaf'), may hold values from -0.375 to 0.375
- leaf_transfer: float32 [1024, 128, 128], P('leaf'), may hold values from -0.1875 to 0.1875
- node_transfer: float32 [128, 128, 128], P('leaf'), may hold values from -0.1875 to 0.1875
- leaf_coupling: float32 [1024, 8, 128, 128], P('leaf', None, 'col'), may hold values from -0.1875 to 0.1875
- node_coupling: float32 [128, 2, 128, 128], P('leaf', None, 'col'), may hold values from -0.375 to 0.375
- top_coupling: float32 [16, 4, 128, 128], P(None, None, 'col'), may hold values from -0.25 to 0.25
- near_list: int32 [1024, 8], P('leaf'), may hold values from -1 to 1023, as said below
- leaf_list: int32 [1024, 8], P('leaf'), may hold values from -1 to 1023, as said below
- node_list: int32 [128, 2], P('leaf'), may hold values from -1 to 127, as said below
- top_list: int32 [16, 4], replicated, may hold values from -1 to 15, as said below
Outputs:
- adjoint_product: float32 [32, 262144], P('col', 'leaf')
Inputs may be any that keep to these rules, and one draw needn't show every extreme that they name: `leaf_list`: leaf l names only leaves other than itself on devices l // 8 - 1 to l // 8 + 1 of a Morton order of 8 leaves a device; slot 0 is live, live slots come first, and some leaf fills all 8 slots. `near_list`: leaf l names only leaves (itself allowed) on devices l // 8 - 1 to l // 8 + 1; slot 0 is live, live slots come first, and some leaf fills all 8 slots. `node_list`: node p names only nodes p - 1 and p + 1; slot 0 is live, live slots come first, and some node fills all 2 slots. `top_list`: top node g may name any top node, itself allowed; slot 0 is live, live slots come first, and some top node fills all 4 slots.
All inputs are finite; a program needn't handle non-finite values.
Results may differ from a plain program's by a relative error of at most 0.0003.
Values sent between devices are 32-bit elements; how exact they have to be, the bound alone decides.
A program may use at most 64 MiB of HBM per device.

v0:
```python
import math
import jax
import jax.numpy as jnp
from jax import lax
from jax.sharding import PartitionSpec as P

SOFTENING = 0.01


def extended_2(x, sides, width):
    for axis, dim in sides:
        devices, length = (lax.axis_size(axis), x.shape[dim])
        up = [(i, (i + 1) % devices) for i in range(devices - 1)]
        down = [(j, i) for i, j in up]
        last = lax.slice_in_dim(x, length - width, length, axis=dim)
        leading = lax.slice_in_dim(x, 0, width, axis=dim)
        before = lax.ppermute(last, axis, up)
        after = lax.ppermute(leading, axis, down)
        x = jnp.concatenate([before, x, after], axis=dim)
    return x


def couple(blocks, local_index, sources):
    high = lax.Precision.HIGHEST
    live_mask = (local_index >= 0).astype(jnp.float32)
    safe_index = jnp.maximum(local_index, 0)
    wide_moments = lax.all_gather(sources, "col", axis=1, tiled=True)
    half_rank = blocks.shape[2]
    rank_start = lax.axis_index("col") * half_rank
    rank_part = lax.dynamic_slice_in_dim(wide_moments, rank_start, half_rank, 2)
    picked = jnp.take(rank_part, safe_index, axis=0) * live_mask[:, :, None, None]
    partial_value = jnp.einsum("nsca,nsab->ncb", picked, blocks, precision=high)
    return lax.psum_scatter(partial_value, "col", scatter_dimension=1, tiled=True)


def body(
    coords,
    values,
    leaf_basis,
    leaf_transfer,
    node_transfer,
    leaf_coupling,
    node_coupling,
    top_coupling,
    near_list,
    leaf_list,
    node_list,
    top_list,
):
    high = lax.Precision.HIGHEST
    device = lax.axis_index("leaf")
    per_device = leaf_basis.shape[0]
    points = leaf_basis.shape[1]
    core_cols = values.shape[0]
    rank_width = leaf_basis.shape[2]
    leaf_values = values.reshape(core_cols, per_device, points)
    leaf_moments = jnp.einsum("lpr,clp->lcr", leaf_basis, leaf_values, precision=high)
    node_moments = jnp.einsum("lab,lca->cb", leaf_transfer, leaf_moments, precision=high)[None]
    contrib = jnp.einsum("nab,nca->ncb", node_transfer, node_moments, precision=high)
    top_count = lax.axis_size("leaf") // 8
    everything = lax.all_gather(contrib, "leaf", axis=0, tiled=True)
    top_moments = everything.reshape(top_count, 8, core_cols, rank_width).sum(axis=1)
    top_node = device // 8
    top_rows = lax.dynamic_slice_in_dim(top_coupling, top_node, 1, 0)
    top_index = lax.dynamic_slice_in_dim(top_list, top_node, 1, 0)
    top_local = couple(top_rows, top_index, top_moments)
    node_ext = extended_2(node_moments, (("leaf", 0),), 1)
    node_index = jnp.where(node_list >= 0, node_list - (device - 1), -1)
    node_local = couple(node_coupling, node_index, node_ext) + jnp.einsum(
        "nab,ncb->nca", node_transfer, top_local, precision=high
    )
    leaf_ext = extended_2(leaf_moments, (("leaf", 0),), per_device)
    leaf_index = jnp.where(leaf_list >= 0, leaf_list - (device - 1) * per_device, -1)
    leaf_local = couple(leaf_coupling, leaf_index, leaf_ext) + jnp.einsum(
        "lab,cb->lca", leaf_transfer, node_local[0], precision=high
    )
    far_field = jnp.einsum("lpr,lcr->clp", leaf_basis, leaf_local, precision=high)
    leaf_rows = jnp.concatenate((coords, values), axis=0)
    extended = extended_2(leaf_rows, (("leaf", 1),), per_device * points)
    extended = extended.reshape(3 + core_cols, 3 * per_device, points)
    near_index = jnp.where(near_list >= 0, near_list - (device - 1) * per_device, -1)
    target = coords.reshape(3, per_device, points)
    scale = 1.0 / math.sqrt(points)
    near_field = jnp.zeros((per_device, core_cols, points), jnp.float32)
    for slot_index in range(near_list.shape[1]):
        column = near_index[:, slot_index]
        live_mask = (column >= 0).astype(jnp.float32)
        source_rows = jnp.take(extended, jnp.maximum(column, 0), axis=1)
        offset_sq = jnp.sum((target[:, :, :, None] - source_rows[:3, :, None, :]) ** 2, axis=0)
        kernel = scale / jnp.sqrt(offset_sq + SOFTENING)
        term = jnp.einsum("lab,clb->lca", kernel, source_rows[3:], precision=high)
        near_field = near_field + live_mask[:, None, None] * term
    total = jnp.transpose(near_field, (1, 0, 2)) + far_field
    return total.reshape(core_cols, per_device * points)


def solution(mesh):
    in_specs = (
        P(None, "leaf"),
        P("col", "leaf"),
        P("leaf", None, None),
        P("leaf", None, None),
        P("leaf", None, None),
        P("leaf", None, "col", None),
        P("leaf", None, "col", None),
        P(None, None, "col", None),
        P("leaf", None),
        P("leaf", None),
        P("leaf", None),
        P(),
    )
    out_specs = P("col", "leaf")
    return jax.shard_map(body, mesh=mesh, in_specs=in_specs, out_specs=out_specs, check_vma=False)
```

profile of v0, /device:TPU:1, one launch (start us, length us, event | category | flops | bytes accessed | tf_op | source)
XLA Modules:
  0.0 207.8 jit_solution(12631651173582469412)
XLA Ops:
  7.5 1.8 pad_maximum_fusion.1
  9.2 5.0 %collective-permute-start = (f32[19,2048]{1,0:T(8,128)}, f32[19,2048]{1,0:T(8,128)}, u32[]{:S(2)}, u32[]{:S(2)}) collective-permute-start(f32[19,2048]{1,0:T(8,128)} %pad_maximum_fusion.1), channel_id=1, source_target_pairs={{0,2},{2,4},{4,6},{6,8},{8,10},{10,12},{12,14},{14,16},{16,18},{18... | collective-permute-start | bytes 466952 | tf_op jit(solution)/shard_map/ppermute | solution.py:17
  15.5 1.9 fusion.107
  17.5 1.4 fusion.159
  18.9 4.0 %collective-permute-start.4 = (f32[1,16,128]{2,1,0:T(8,128)S(1)}, f32[1,16,128]{2,1,0:T(8,128)S(1)}, u32[]{:S(2)}, u32[]{:S(2)}) collective-permute-start(f32[1,16,128]{2,1,0:T(8,128)S(1)} %bitcast.94), channel_id=1, source_target_pairs={{0,2},{2,4},{4,6},{6,8},{8,10},{10,12},{12,14},{14,16},{16,18},{18... | collective-permute-start | bytes 24584 | tf_op jit(solution)/shard_map/ppermute | solution.py:17
  24.2 4.0 %collective-permute-start.2 = (f32[8,16,128]{2,1,0:T(8,128)S(1)}, f32[8,16,128]{2,1,0:T(8,128)S(1)}, u32[]{:S(2)}, u32[]{:S(2)}) collective-permute-start(f32[8,16,128]{2,1,0:T(8,128)S(1)} %fusion.107), channel_id=1, source_target_pairs={{0,2},{2,4},{4,6},{6,8},{8,10},{10,12},{12,14},{14,16},{16,18},{18... | collective-permute-start | bytes 196616 | tf_op jit(solution)/shard_map/ppermute | solution.py:17
  41.6 3.6 %all_gather.13 = f32[3,32,128]{2,1,0:T(8,128)S(1)} all-gather(f32[3,16,128]{2,1,0:T(8,128)S(1)} %pad_maximum_fusion.3), channel_id=1, replica_groups=mesh['leaf'=128,'col'=2] {'col'}, dimensions={1}, use_global_device_ids=true | all-gather | bytes 73728 | tf_op jit(solution)/shard_map/all_gather | solution.py:27
  46.8 3.7 %all_gather.12 = f32[24,32,128]{2,1,0:T(8,128)S(1)} all-gather(f32[24,16,128]{2,1,0:T(8,128)S(1)} %pad_maximum_fusion.2), channel_id=1, replica_groups=mesh['leaf'=128,'col'=2] {'col'}, dimensions={1}, use_global_device_ids=true | all-gather | bytes 589824 | tf_op jit(solution)/shard_map/all_gather | solution.py:27
  51.3 84.4 %all-gather.3.cloned.1.call-done = f32[2048,128]{1,0:T(8,128)} async-done(((f32[16,128]{1,0:T(8,128)}), f32[2048,128]{1,0:T(8,128)}) %all-gather.3.cloned.1.call-update) | async-done | bytes 1048592 | tf_op jit(solution)/shard_map/all_gather | solution.py:61
  135.7 1.3 reduce_sum.89
  137.0 7.1 %all_gather.15 = f32[16,32,128]{2,1,0:T(8,128)S(1)} all-gather(f32[16,16,128]{2,1,0:T(8,128)S(1)} %reduce_sum.89), channel_id=1, replica_groups=mesh['leaf'=128,'col'=2] {'col'}, dimensions={1}, use_global_device_ids=true | all-gather | bytes 393216 | tf_op jit(solution)/shard_map/all_gather | solution.py:27
  144.3 1.3 gather_fusion.2
  145.6 1.9 convolution_bitcast_fusion.2
  147.5 2.1 %convolution_bitcast_fusion = f32[8,32,128]{2,1,0:T(8,128)} fusion(f32[8,8,64,128]{3,2,1,0:T(8,128)S(1)} %copy-done, f32[8,8,32,64]{3,2,1,0:T(8,128)S(1)} %bitcast.87, f32[8,8]{1,0:T(8,128)S(1)} %get-tuple-element.34, pred[8,8]{1,0:T(8,128)(4,1)S(1)} %copy-done.17), kind=kOutput, calls=%fused_computation.68 | convolution fusion | flops 201588736 | bytes 2752832 | tf_op jit(solution)/shard_map/nsca,nsab->ncb/dot_general | solution.py:32
  167.2 11.0 %multiply_reduce_fusion = (f32[8,256,256]{2,1,0:T(8,128)}, f32[8,256,256]{2,1,0:T(8,128)S(1)}, f32[8,256,256]{2,1,0:T(8,128)S(1)}, f32[8,256,256]{2,1,0:T(8,128)...) fusion(f32[3,8,256]{2,1,0:T(8,128)S(1)} %copy.65, ...), kind=kLoop, calls=%fused_computation.11 | loop fusion | flops 33554432 | bytes 16998400 | tf_op jit(solution)/shard_map/reduce_sum | solution.py:89
  178.3 1.9 fusion.44
  180.2 1.9 fusion.47
  182.1 1.9 fusion.50
  184.1 1.9 fusion.65
  186.0 1.9 fusion.68
  187.9 1.9 fusion.41
  189.9 2.6 %fusion.62 = f32[8,16,256]{2,1,0:T(8,128)} fusion(f32[8,16,256]{2,1,0:T(8,128)S(1)} %fusion.68, f32[8,16,256]{2,1,0:T(8,128)S(1)} %fusion.65, f32[8,16,256]{2,1,0:T(8,128)S(1)} %fusion.41, f32[8,256,256]{2,1,0:T(8,128)S(1)} %get-tuple-element.10, f32[19,8,256]{2,0,1:T(8,128)S(1)} %select_bitcast_fusion.3, f32[8]{0:T(128)S(1)} %copy-done.20), kind=kOutput, calls=%fused_computation.61 | convolution fusion | flops 101842944 | bytes 2753024 | tf_op jit(solution)/shard_map/lab,clb->lca/dot_general | solution.py:91
  193.5 1.6 fusion.83
  196.1 3.5 %fusion.80 = f32[8,2,8,256]{3,2,1,0:T(8,128)S(1)} fusion(f32[8,16,256]{2,1,0:T(8,128)S(1)} %fusion.160, f32[8,16,256]{2,1,0:T(8,128)} %fusion.62, f32[8,256,256]{2,1,0:T(8,128)} %get-tuple-element.6, f32[19,8,256]{2,0,1:T(8,128)S(1)} %select_bitcast_fusion, f32[8]{0:T(128)S(1)} %copy-done.32), kind=kOutput, calls=%fused_computation.67 | convolution fusion | flops 101810176 | bytes 2621952 | tf_op jit(solution)/shard_map/lab,clb->lca/dot_general | solution.py:91
  (168 shorter events, 38.5 us)
Async XLA Ops:
  7.4 140.1 %copy-start = (f32[8,8,64,128]{3,2,1,0:T(8,128)S(1)}, f32[8,8,64,128]{3,2,1,0:T(8,128)}, u32[]{:S(2)}) copy-start(f32[8,8,64,128]{3,2,1,0:T(8,128)} %param.19) | copy-start | bytes 6291460
  7.4 30.8 %copy-start.11 = (f32[3,2048]{1,0:T(4,128)S(1)}, f32[3,2048]{1,0:T(4,128)}, u32[]{:S(2)}) copy-start(f32[3,2048]{1,0:T(4,128)} %param.14) | copy-start | bytes 73732
  7.4 20.8 %copy-start.13 = (f32[1,128,128]{2,1,0:T(8,128)S(1)}, f32[1,128,128]{2,1,0:T(8,128)}, u32[]{:S(2)}) copy-start(f32[1,128,128]{2,1,0:T(8,128)} %param.18) | copy-start | bytes 196612
  7.4 21.7 %copy-start.19 = (s32[8,8]{1,0:T(8,128)S(1)}, s32[8,8]{1,0:T(8,128)}, u32[]{:S(2)}) copy-start(s32[8,8]{1,0:T(8,128)} %param.22) | copy-start | bytes 772
  7.4 25.6 %copy-start.16 = (s32[16,4]{0,1:T(4,128)S(1)}, s32[16,4]{0,1:T(4,128)}, u32[]{:S(2)}) copy-start(s32[16,4]{0,1:T(4,128)} %param.25) | copy-start | bytes 772
  7.4 26.4 %copy-start.33 = (s32[1,2]{1,0:T(1,128)S(1)}, s32[1,2]{1,0:T(1,128)}, u32[]{:S(2)}) copy-start(s32[1,2]{1,0:T(1,128)} %param.24) | copy-start | bytes 28
  7.4 26.4 %copy-start.18 = (s32[8,8]{1,0:T(8,128)S(1)}, s32[8,8]{1,0:T(8,128)}, u32[]{:S(2)}) copy-start(s32[8,8]{1,0:T(8,128)} %param.23) | copy-start | bytes 772
  7.4 38.4 %copy-start.15 = (f32[1,2,64,128]{3,2,1,0:T(8,128)S(1)}, f32[1,2,64,128]{3,2,1,0:T(8,128)}, u32[]{:S(2)}) copy-start(f32[1,2,64,128]{3,2,1,0:T(8,128)} %param.20) | copy-start | bytes 196612
  7.4 128.3 %all-gather.3.cloned.1.call-start = ((), (), s32[]{:S(2)}) async-start(), calls=%async_computation.6 | async-start | bytes 1056768 | tf_op jit(solution)/shard_map/all_gather | solution.py:61
  9.2 140.5 %collective-permute-start = (f32[19,2048]{1,0:T(8,128)}, f32[19,2048]{1,0:T(8,128)}, u32[]{:S(2)}, u32[]{:S(2)}) collective-permute-start(f32[19,2048]{1,0:T(8,128)} %pad_maximum_fusion.1), channel_id=1, source_target_pairs={{0,2},{2,4},{4,6},{6,8},{8,10},{10,12},{12,14},{14,16},{16,18},{18... | collective-permute-start | bytes 466952 | tf_op jit(solution)/shard_map/ppermute | solution.py:17
  14.3 135.5 %collective-permute-start.1 = (f32[19,2048]{1,0:T(8,128)}, f32[19,2048]{1,0:T(8,128)}, u32[]{:S(2)}, u32[]{:S(2)}) collective-permute-start(f32[19,2048]{1,0:T(8,128)} %pad_maximum_fusion.1), channel_id=1, source_target_pairs={{2,0},{4,2},{6,4},{8,6},{10,8},{12,10},{14,12},{16,14},{18,16},{20... | collective-permute-start | bytes 466952 | tf_op jit(solution)/shard_map/ppermute | solution.py:18
  18.9 21.4 %collective-permute-start.4 = (f32[1,16,128]{2,1,0:T(8,128)S(1)}, f32[1,16,128]{2,1,0:T(8,128)S(1)}, u32[]{:S(2)}, u32[]{:S(2)}) collective-permute-start(f32[1,16,128]{2,1,0:T(8,128)S(1)} %bitcast.94), channel_id=1, source_target_pairs={{0,2},{2,4},{4,6},{6,8},{8,10},{10,12},{12,14},{14,16},{16,18},{18... | collective-permute-start | bytes 24584 | tf_op jit(solution)/shard_map/ppermute | solution.py:17
  22.9 18.7 %collective-permute-start.5 = (f32[1,16,128]{2,1,0:T(8,128)S(1)}, f32[1,16,128]{2,1,0:T(8,128)S(1)}, u32[]{:S(2)}, u32[]{:S(2)}) collective-permute-start(f32[1,16,128]{2,1,0:T(8,128)S(1)} %bitcast.95), channel_id=1, source_target_pairs={{2,0},{4,2},{6,4},{8,6},{10,8},{12,10},{14,12},{16,14},{18,16},{20... | collective-permute-start | bytes 24584 | tf_op jit(solution)/shard_map/ppermute | solution.py:18
  24.2 22.6 %collective-permute-start.2 = (f32[8,16,128]{2,1,0:T(8,128)S(1)}, f32[8,16,128]{2,1,0:T(8,128)S(1)}, u32[]{:S(2)}, u32[]{:S(2)}) collective-permute-start(f32[8,16,128]{2,1,0:T(8,128)S(1)} %fusion.107), channel_id=1, source_target_pairs={{0,2},{2,4},{4,6},{6,8},{8,10},{10,12},{12,14},{14,16},{16,18},{18... | collective-permute-start | bytes 196616 | tf_op jit(solution)/shard_map/ppermute | solution.py:17
  29.0 163.4 %reduce-scatter.6.cloned.1.call-start = ((), (), s32[]{:S(2)}) async-start(), calls=%async_computation.4 | async-start | bytes 24576 | tf_op jit(solution)/shard_map/reduce_scatter | solution.py:33
  40.3 6.5 %collective-permute-start.3 = (f32[8,16,128]{2,1,0:T(8,128)S(1)}, f32[8,16,128]{2,1,0:T(8,128)S(1)}, u32[]{:S(2)}, u32[]{:S(2)}) collective-permute-start(f32[8,16,128]{2,1,0:T(8,128)S(1)} %fusion.107), channel_id=1, source_target_pairs={{2,0},{4,2},{6,4},{8,6},{10,8},{12,10},{14,12},{16,14},{18,16},{20... | collective-permute-start | bytes 196616 | tf_op jit(solution)/shard_map/ppermute | solution.py:18
  46.7 145.7 %reduce-scatter.8.cloned.1.call-start = ((), (), s32[]{:S(2)}) async-start(), calls=%async_computation.5 | async-start | bytes 24576 | tf_op jit(solution)/shard_map/reduce_scatter | solution.py:33
  51.3 96.2 %copy-start.17 = (pred[8,8]{1,0:T(8,128)(4,1)S(1)}, pred[8,8]{1,0:T(8,128)(4,1)}, u32[]{:S(2)}) copy-start(pred[8,8]{1,0:T(8,128)(4,1)} %get-tuple-element.32) | copy-start | bytes 196
  147.5 46.0 %reduce-scatter.4.cloned.1.call-start = ((), (), s32[]{:S(2)}) async-start(), calls=%async_computation.3 | async-start | bytes 196608 | tf_op jit(solution)/shard_map/reduce_scatter | solution.py:33
  151.1 7.8 %copy-start.28 = (pred[8]{0:T(512)(128)(4,1)S(1)}, pred[8]{0:T(512)(128)(4,1)}, u32[]{:S(2)}) copy-start(pred[8]{0:T(512)(128)(4,1)} %get-tuple-element.44) | copy-start | bytes 28
  152.0 9.0 %copy-start.27 = (pred[8]{0:T(512)(128)(4,1)S(1)}, pred[8]{0:T(512)(128)(4,1)}, u32[]{:S(2)}) copy-start(pred[8]{0:T(512)(128)(4,1)} %get-tuple-element.43) | copy-start | bytes 28
  155.6 11.6 %copy-start.14 = (f32[1,3,8,256]{3,2,1,0:T(8,128)S(1)}, f32[1,3,8,256]{3,2,1,0:T(8,128)}, u32[]{:S(2)}) copy-start(f32[1,3,8,256]{3,2,1,0:T(8,128)} %copy.78) | copy-start | bytes 73732
  167.2 11.0 %copy-start.26 = (f32[8]{0:T(128)S(1)}, f32[8]{0:T(128)}, u32[]{:S(2)}) copy-start(f32[8]{0:T(128)} %get-tuple-element.20) | copy-start | bytes 100
  189.8 6.2 %copy-start.32 = (f32[8]{0:T(128)S(1)}, f32[8]{0:T(128)}, u32[]{:S(2)}) copy-start(f32[8]{0:T(128)} %get-tuple-element.14) | copy-start | bytes 100
  (20 other events, 62.9 us)
Sparse Core Ops, SparseCore 0:
  29.1 106.5 all-gather.2
Sparse Core Ops, SparseCore 1:
  46.8 21.7 reduce-scatter.5
  147.5 12.2 reduce-scatter.7
  162.2 14.1 reduce-scatter.3
where the time goes:
time: 209 us; the launch traced here: 208 us
  waiting for transfers between devices  84.5 us (40%)
  matrix products  30 us (14%)
  other arithmetic  28.5 us (14%)
  local copies, waits for them, and re-layouts  17.6 us (8%)
  starting transfers between devices  17 us (8%)
  between operations  15.8 us (8%)
  blocking collectives  14.3 us (7%)
    all_gather x1, waiting for transfers between devices, body(): everything = lax.all_gather(contrib, 'leaf', axis=0, tiled=True)  84.4 us
    dot_general x8, matrix products, body(): term = jnp.einsum('lab,clb->lca', kernel, source_rows[3:], precision=high)  17.4 us
    all_gather x3, blocking collectives, couple(): wide_moments = lax.all_gather(sources, 'col', axis=1, tiled=True)  14.3 us
    ppermute x3, starting transfers between devices, extended_2(): before = lax.ppermute(last, axis, up)  13 us
    reduce_sum x1, other arithmetic, body(): jnp.sum((target[:, :, :, None] - source_rows[:3, :, None, :]) ** 2, axis=0)  11 us
    gather x8, local copies, waits for them, and re-layouts, body(): source_rows = jnp.take(extended, jnp.maximum(column, 0), axis=1)  5.88 us
    dot_general x3, matrix products, couple(): partial_value = jnp.einsum('nsca,nsab->ncb', picked, blocks, precision=high)  4.92 us
    slice x16, local copies, waits for them, and re-layouts, body(): source_rows[:3, :, None, :]  4.28 us
  transfers between devices with their start and end apart: 10, of which 2 were waited for; matrix products, arithmetic and copies ran while one was open for 31% of the time, Pallas kernels for 0%

commit v1 on v0

--- a/solution.py
+++ b/solution.py
@@ -58,7 +58,9 @@
     node_moments = jnp.einsum("lab,lca->cb", leaf_transfer, leaf_moments, precision=high)[None]
     contrib = jnp.einsum("nab,nca->ncb", node_transfer, node_moments, precision=high)
     top_count = lax.axis_size("leaf") // 8
-    everything = lax.all_gather(contrib, "leaf", axis=0, tiled=True)
+    everything = jnp.concatenate(
+        lax.all_to_all(jnp.stack([contrib] * lax.axis_size("leaf")), "leaf", 0, 0), axis=0
+    )
     top_moments = everything.reshape(top_count, 8, core_cols, rank_width).sum(axis=1)
     top_node = device // 8
     top_rows = lax.dynamic_slice_in_dim(top_coupling, top_node, 1, 0)

time: 209 us -> 148 us (0.71)
  waiting for transfers between devices: 84.5 us -> 5.81 us
  starting transfers between devices: 17 us -> 37.7 us
    all_gather x1 -> x0, waiting for transfers between devices: 84.4 us -> none  [body(): everything = lax.all_gather(contrib, 'leaf', axis=0, tiled=True)]
    all_to_all x0 -> x1, starting transfers between devices: none -> 20.7 us  [body(): lax.all_to_all(jnp.stack([contrib] * lax.axis_size('leaf')), 'leaf', 0, 0)]
    ppermute x3, waiting for transfers between devices: 0.01 us -> 4.53 us  [extended_2(): after = lax.ppermute(leading, axis, down)]
  transfers between devices with their start and end apart: 10 -> 10, of which waited for: 2 -> 3; matrix products, arithmetic and copies ran while one was open for 31% -> 44% of each run, Pallas kernels for 0% -> 0%
where the time goes in v1:
time: 148 us; the launch traced here: 147 us
  starting transfers between devices  37.7 us (25%)
  matrix products  29.4 us (20%)
  other arithmetic  28.4 us (19%)
  local copies, waits for them, and re-layouts  18.8 us (13%)
  between operations  13.9 us (9%)
  blocking collectives  13.5 us (9%)
  waiting for transfers between devices  5.81 us (4%)
    all_to_all x1, starting transfers between devices, body(): lax.all_to_all(jnp.stack([contrib] * lax.axis_size('leaf')), 'leaf', 0, 0)  20.7 us
    dot_general x8, matrix products, body(): term = jnp.einsum('lab,clb->lca', kernel, source_rows[3:], precision=high)  17.4 us
    all_gather x3, blocking collectives, couple(): wide_moments = lax.all_gather(sources, 'col', axis=1, tiled=True)  13.5 us
    ppermute x3, starting transfers between devices, extended_2(): before = lax.ppermute(last, axis, up)  13 us
    reduce_sum x1, other arithmetic, body(): jnp.sum((target[:, :, :, None] - source_rows[:3, :, None, :]) ** 2, axis=0)  11 us
    gather x8, local copies, waits for them, and re-layouts, body(): source_rows = jnp.take(extended, jnp.maximum(column, 0), axis=1)  5.88 us
    dot_general x3, matrix products, couple(): partial_value = jnp.einsum('nsca,nsab->ncb', picked, blocks, precision=high)  4.91 us
    ppermute x3, waiting for transfers between devices, extended_2(): after = lax.ppermute(leading, axis, down)  4.53 us
  transfers between devices with their start and end apart: 10, of which 3 were waited for; matrix products, arithmetic and copies ran while one was open for 44% of the time, Pallas kernels for 0%

profile of v1, /device:TPU:1, one launch (start us, length us, event | category | flops | bytes accessed | tf_op | source)
XLA Modules:
  0.0 147.4 jit_solution(2955768676463069127)
XLA Ops:
  6.5 1.8 %pad_maximum_fusion.1 = f32[19,2048]{1,0:T(8,128)} fusion(f32[16,2048]{1,0:T(8,128)} %param.15, f32[3,2048]{1,0:T(4,128)} %param.14), kind=kLoop, calls=%fused_computation.99 | loop fusion | flops 38912 | bytes 311296 | tf_op jit(solution)/shard_map/concatenate | solution.py:80
  8.3 5.0 %collective-permute-start = (f32[19,2048]{1,0:T(8,128)}, f32[19,2048]{1,0:T(8,128)}, u32[]{:S(2)}, u32[]{:S(2)}) collective-permute-start(f32[19,2048]{1,0:T(8,128)} %pad_maximum_fusion.1), channel_id=1, source_target_pairs={{0,2},{2,4},{4,6},{6,8},{8,10},{10,12},{12,14},{14,16},{16,18},{18... | collective-permute-start | bytes 466952 | tf_op jit(solution)/shard_map/ppermute | solution.py:17
  14.6 1.9 %fusion.107 = f32[8,16,128]{2,1,0:T(8,128)S(1)} fusion(f32[8,256,128]{2,1,0:T(8,128)} %param.16, f32[2,8,8,256]{3,2,1,0:T(8,128)} %bitcast.92), kind=kOutput, calls=%fused_computation.109 | convolution fusion | flops 50331648 | bytes 1245184 | tf_op jit(solution)/shard_map/lpr,clp->lcr/dot_general | solution.py:57
  16.6 1.4 fusion.159
  18.1 4.0 %collective-permute-start.4 = (f32[1,16,128]{2,1,0:T(8,128)S(1)}, f32[1,16,128]{2,1,0:T(8,128)S(1)}, u32[]{:S(2)}, u32[]{:S(2)}) collective-permute-start(f32[1,16,128]{2,1,0:T(8,128)S(1)} %bitcast.95), channel_id=1, source_target_pairs={{0,2},{2,4},{4,6},{6,8},{8,10},{10,12},{12,14},{14,16},{16,18},{18... | collective-permute-start | bytes 24584 | tf_op jit(solution)/shard_map/ppermute | solution.py:17
  23.4 4.0 %collective-permute-start.2 = (f32[8,16,128]{2,1,0:T(8,128)S(1)}, f32[8,16,128]{2,1,0:T(8,128)S(1)}, u32[]{:S(2)}, u32[]{:S(2)}) collective-permute-start(f32[8,16,128]{2,1,0:T(8,128)S(1)} %fusion.107), channel_id=1, source_target_pairs={{0,2},{2,4},{4,6},{6,8},{8,10},{10,12},{12,14},{14,16},{16,18},{18... | collective-permute-start | bytes 196616 | tf_op jit(solution)/shard_map/ppermute | solution.py:17
  28.7 20.7 %all-to-all-start = ((f32[128,1,16,128]{3,2,1,0:T(8,128)}), f32[128,1,16,128]{3,2,1,0:T(8,128)}, u32[]{:S(2)}, u32[]{:S(2)}) async-start(f32[128,1,16,128]{3,2,1,0:T(8,128)} %stack.2), calls=%async_computation.2 | async-start | bytes 2097152 | tf_op jit(solution)/shard_map/all_to_all | solution.py:62
  61.8 3.6 %all_gather.10 = f32[3,32,128]{2,1,0:T(8,128)S(1)} all-gather(f32[3,16,128]{2,1,0:T(8,128)S(1)} %pad_maximum_fusion.3), channel_id=1, replica_groups=mesh['leaf'=128,'col'=2] {'col'}, dimensions={1}, use_global_device_ids=true | all-gather | bytes 73728 | tf_op jit(solution)/shard_map/all_gather | solution.py:27
  67.0 4.5 %collective-permute-done.3 = f32[8,16,128]{2,1,0:T(8,128)S(1)} collective-permute-done((f32[8,16,128]{2,1,0:T(8,128)S(1)}, f32[8,16,128]{2,1,0:T(8,128)S(1)}, u32[]{:S(2)}, u32[]{:S(2)}) %collective-permute-start.3) | collective-permute-done | bytes 65568 | tf_op jit(solution)/shard_map/ppermute | solution.py:18
  71.6 4.4 %all_gather.9 = f32[24,32,128]{2,1,0:T(8,128)S(1)} all-gather(f32[24,16,128]{2,1,0:T(8,128)S(1)} %pad_maximum_fusion.2), channel_id=1, replica_groups=mesh['leaf'=128,'col'=2] {'col'}, dimensions={1}, use_global_device_ids=true | all-gather | bytes 589824 | tf_op jit(solution)/shard_map/all_gather | solution.py:27
  79.3 5.5 %all_gather.11 = f32[16,32,128]{2,1,0:T(8,128)S(1)} all-gather(f32[16,16,128]{2,1,0:T(8,128)S(1)} %bitcast_reduce_fusion), channel_id=1, replica_groups=mesh['leaf'=128,'col'=2] {'col'}, dimensions={1}, use_global_device_ids=true | all-gather | bytes 393216 | tf_op jit(solution)/shard_map/all_gather | solution.py:27
  84.9 1.3 gather_fusion.2
  86.2 1.9 %convolution_bitcast_fusion.2 = f32[1,32,128]{2,1,0:T(8,128)} fusion(f32[16,4,64,128]{3,2,1,0:T(8,128)} %param.21, s32[]{:T(128)S(6)} %select_n.66, f32[4,32,64]{2,1,0:T(8,128)} %gather_fusion.2, f32[4]{0:T(128)} %convert_reduce_fusion.8, pred[4]{0:T(512)(128)(4,1)} %compare_reduce_fusion), kind=kOutput, calls=%fused_computation.71 | convolution fusion | flops 12599296 | bytes 214020 | tf_op jit(solution)/shard_map/nsca,nsab->ncb/dot_general | solution.py:32
  88.2 2.1 %convolution_bitcast_fusion = f32[8,32,128]{2,1,0:T(8,128)} fusion(f32[8,8,64,128]{3,2,1,0:T(8,128)S(1)} %copy-done, f32[8,8,32,64]{3,2,1,0:T(8,128)S(1)} %bitcast.89, f32[8,8]{1,0:T(8,128)S(1)} %get-tuple-element.34, pred[8,8]{1,0:T(8,128)(4,1)S(1)} %copy-done.17), kind=kOutput, calls=%fused_computation.68 | convolution fusion | flops 201588736 | bytes 2752832 | tf_op jit(solution)/shard_map/nsca,nsab->ncb/dot_general | solution.py:32
  107.9 11.0 %multiply_reduce_fusion = (f32[8,256,256]{2,1,0:T(8,128)}, f32[8,256,256]{2,1,0:T(8,128)S(1)}, f32[8,256,256]{2,1,0:T(8,128)S(1)}, f32[8,256,256]{2,1,0:T(8,128)...) fusion(f32[3,8,256]{2,1,0:T(8,128)S(1)} %copy.83, ...), kind=kLoop, calls=%fused_computation.11 | loop fusion | flops 33554432 | bytes 16998400 | tf_op jit(solution)/shard_map/reduce_sum | solution.py:91
  118.9 1.9 %fusion.44 = f32[8,16,256]{2,1,0:T(8,128)S(1)} fusion(f32[8,256,256]{2,1,0:T(8,128)S(1)} %get-tuple-element.7, f32[19,8,256]{2,0,1:T(8,128)S(1)} %select_bitcast_fusion.6, f32[8]{0:T(128)S(1)} %copy-done.26), kind=kOutput, calls=%fused_computation.55 | convolution fusion | flops 101744640 | bytes 2359808 | tf_op jit(solution)/shard_map/lab,clb->lca/dot_general | solution.py:93
  120.8 1.9 %fusion.47 = f32[8,16,256]{2,1,0:T(8,128)S(1)} fusion(f32[8,256,256]{2,1,0:T(8,128)S(1)} %get-tuple-element.8, f32[19,8,256]{2,0,1:T(8,128)S(1)} %select_bitcast_fusion.5, f32[8]{0:T(128)S(1)} %copy-done.25), kind=kOutput, calls=%fused_computation.56 | convolution fusion | flops 101744640 | bytes 2359808 | tf_op jit(solution)/shard_map/lab,clb->lca/dot_general | solution.py:93
  122.8 1.9 %fusion.50 = f32[8,16,256]{2,1,0:T(8,128)S(1)} fusion(f32[8,256,256]{2,1,0:T(8,128)S(1)} %get-tuple-element.9, f32[19,8,256]{2,0,1:T(8,128)S(1)} %copy-done.4, f32[8]{0:T(128)S(1)} %copy-done.24), kind=kOutput, calls=%fused_computation.57 | convolution fusion | flops 101744640 | bytes 2359808 | tf_op jit(solution)/shard_map/lab,clb->lca/dot_general | solution.py:93
  124.7 1.9 %fusion.65 = f32[8,16,256]{2,1,0:T(8,128)S(1)} fusion(f32[8,256,256]{2,1,0:T(8,128)S(1)} %get-tuple-element.11, f32[19,8,256]{2,0,1:T(8,128)S(1)} %copy-done.6, f32[8]{0:T(128)S(1)} %copy-done.23), kind=kOutput, calls=%fused_computation.62 | convolution fusion | flops 101744640 | bytes 2359808 | tf_op jit(solution)/shard_map/lab,clb->lca/dot_general | solution.py:93
  126.6 1.9 %fusion.68 = f32[8,16,256]{2,1,0:T(8,128)S(1)} fusion(f32[8,256,256]{2,1,0:T(8,128)S(1)} %get-tuple-element.12, f32[19,8,256]{2,0,1:T(8,128)S(1)} %copy-done.8, f32[8]{0:T(128)S(1)} %copy-done.22), kind=kOutput, calls=%fused_computation.63 | convolution fusion | flops 101744640 | bytes 2359808 | tf_op jit(solution)/shard_map/lab,clb->lca/dot_general | solution.py:93
  128.6 1.9 %fusion.41 = f32[8,16,256]{2,1,0:T(8,128)S(1)} fusion(f32[8,16,256]{2,1,0:T(8,128)S(1)} %fusion.50, f32[8,16,256]{2,1,0:T(8,128)S(1)} %fusion.47, f32[8,16,256]{2,1,0:T(8,128)S(1)} %fusion.44, f32[8,256,256]{2,1,0:T(8,128)S(1)} %get-tuple-element.13, f32[19,8,256]{2,0,1:T(8,128)S(1)} %copy-done.10, f32[8]{0:T(128)S(1)} %copy-done.21), kind=kOutput, calls=%fused_computation.54 | convolution fusion | flops 101842944 | bytes 2753024 | tf_op jit(solution)/shard_map/lab,clb->lca/dot_general | solution.py:93
  130.5 2.6 %fusion.62 = f32[8,16,256]{2,1,0:T(8,128)} fusion(f32[8,16,256]{2,1,0:T(8,128)S(1)} %fusion.68, f32[8,16,256]{2,1,0:T(8,128)S(1)} %fusion.65, f32[8,16,256]{2,1,0:T(8,128)S(1)} %fusion.41, f32[8,256,256]{2,1,0:T(8,128)S(1)} %get-tuple-element.10, f32[19,8,256]{2,0,1:T(8,128)S(1)} %select_bitcast_fusion.3, f32[8]{0:T(128)S(1)} %copy-done.20), kind=kOutput, calls=%fused_computation.61 | convolution fusion | flops 101842944 | bytes 2753024 | tf_op jit(solution)/shard_map/lab,clb->lca/dot_general | solution.py:93
  134.1 1.6 %fusion.83 = f32[8,16,128]{2,1,0:T(8,128)S(1)} fusion(f32[8,16,128]{2,1,0:T(8,128)} %reduce-scatter.4.cloned.1.call-done, f32[16,128,1]{1,0,2:T(8,128)S(1)} %fusion.85, f32[8,128,128]{2,1,0:T(8,128)} %param.17), kind=kOutput, calls=%fused_computation.70 | convolution fusion | flops 25182208 | bytes 663552 | tf_op jit(solution)/shard_map/lab,cb->lca/dot_general | solution.py:76
  136.7 3.5 %fusion.80 = f32[8,2,8,256]{3,2,1,0:T(8,128)S(1)} fusion(f32[8,16,256]{2,1,0:T(8,128)S(1)} %fusion.160, f32[8,16,256]{2,1,0:T(8,128)} %fusion.62, f32[8,256,256]{2,1,0:T(8,128)} %get-tuple-element.6, f32[19,8,256]{2,0,1:T(8,128)S(1)} %select_bitcast_fusion, f32[8]{0:T(128)S(1)} %copy-done.32), kind=kOutput, calls=%fused_computation.67 | convolution fusion | flops 101810176 | bytes 2621952 | tf_op jit(solution)/shard_map/lab,clb->lca/dot_general | solution.py:93
  (168 shorter events, 41.3 us)
Async XLA Ops:
  6.5 81.6 %copy-start = (f32[8,8,64,128]{3,2,1,0:T(8,128)S(1)}, f32[8,8,64,128]{3,2,1,0:T(8,128)}, u32[]{:S(2)}) copy-start(f32[8,8,64,128]{3,2,1,0:T(8,128)} %param.19) | copy-start | bytes 6291460
  6.5 20.8 %copy-start.13 = (f32[1,128,128]{2,1,0:T(8,128)S(1)}, f32[1,128,128]{2,1,0:T(8,128)}, u32[]{:S(2)}) copy-start(f32[1,128,128]{2,1,0:T(8,128)} %param.18) | copy-start | bytes 196612
  8.3 82.0 %collective-permute-start = (f32[19,2048]{1,0:T(8,128)}, f32[19,2048]{1,0:T(8,128)}, u32[]{:S(2)}, u32[]{:S(2)}) collective-permute-start(f32[19,2048]{1,0:T(8,128)} %pad_maximum_fusion.1), channel_id=1, source_target_pairs={{0,2},{2,4},{4,6},{6,8},{8,10},{10,12},{12,14},{14,16},{16,18},{18... | collective-permute-start | bytes 466952 | tf_op jit(solution)/shard_map/ppermute | solution.py:17
  13.3 77.0 %collective-permute-start.1 = (f32[19,2048]{1,0:T(8,128)}, f32[19,2048]{1,0:T(8,128)}, u32[]{:S(2)}, u32[]{:S(2)}) collective-permute-start(f32[19,2048]{1,0:T(8,128)} %pad_maximum_fusion.1), channel_id=1, source_target_pairs={{2,0},{4,2},{6,4},{8,6},{10,8},{12,10},{14,12},{16,14},{18,16},{20... | collective-permute-start | bytes 466952 | tf_op jit(solution)/shard_map/ppermute | solution.py:18
  16.6 32.9 %copy-start.19 = (s32[8,8]{1,0:T(8,128)S(1)}, s32[8,8]{1,0:T(8,128)}, u32[]{:S(2)}) copy-start(s32[8,8]{1,0:T(8,128)} %param.22) | copy-start | bytes 772
  16.6 38.2 %copy-start.16 = (s32[16,4]{0,1:T(4,128)S(1)}, s32[16,4]{0,1:T(4,128)}, u32[]{:S(2)}) copy-start(s32[16,4]{0,1:T(4,128)} %param.25) | copy-start | bytes 772
  16.6 39.0 %copy-start.33 = (s32[1,2]{1,0:T(1,128)S(1)}, s32[1,2]{1,0:T(1,128)}, u32[]{:S(2)}) copy-start(s32[1,2]{1,0:T(1,128)} %param.24) | copy-start | bytes 28
  16.6 39.0 %copy-start.18 = (s32[8,8]{1,0:T(8,128)S(1)}, s32[8,8]{1,0:T(8,128)}, u32[]{:S(2)}) copy-start(s32[8,8]{1,0:T(8,128)} %param.23) | copy-start | bytes 772
  16.6 41.9 %copy-start.11 = (f32[3,2048]{1,0:T(4,128)S(1)}, f32[3,2048]{1,0:T(4,128)}, u32[]{:S(2)}) copy-start(f32[3,2048]{1,0:T(4,128)} %param.14) | copy-start | bytes 73732
  16.6 49.4 %copy-start.15 = (f32[1,2,64,128]{3,2,1,0:T(8,128)S(1)}, f32[1,2,64,128]{3,2,1,0:T(8,128)}, u32[]{:S(2)}) copy-start(f32[1,2,64,128]{3,2,1,0:T(8,128)} %param.20) | copy-start | bytes 196612
  18.1 42.4 %collective-permute-start.4 = (f32[1,16,128]{2,1,0:T(8,128)S(1)}, f32[1,16,128]{2,1,0:T(8,128)S(1)}, u32[]{:S(2)}, u32[]{:S(2)}) collective-permute-start(f32[1,16,128]{2,1,0:T(8,128)S(1)} %bitcast.95), channel_id=1, source_target_pairs={{0,2},{2,4},{4,6},{6,8},{8,10},{10,12},{12,14},{14,16},{16,18},{18... | collective-permute-start | bytes 24584 | tf_op jit(solution)/shard_map/ppermute | solution.py:17
  22.1 39.7 %collective-permute-start.5 = (f32[1,16,128]{2,1,0:T(8,128)S(1)}, f32[1,16,128]{2,1,0:T(8,128)S(1)}, u32[]{:S(2)}, u32[]{:S(2)}) collective-permute-start(f32[1,16,128]{2,1,0:T(8,128)S(1)} %bitcast.96), channel_id=1, source_target_pairs={{2,0},{4,2},{6,4},{8,6},{10,8},{12,10},{14,12},{16,14},{18,16},{20... | collective-permute-start | bytes 24584 | tf_op jit(solution)/shard_map/ppermute | solution.py:18
  23.4 43.6 %collective-permute-start.2 = (f32[8,16,128]{2,1,0:T(8,128)S(1)}, f32[8,16,128]{2,1,0:T(8,128)S(1)}, u32[]{:S(2)}, u32[]{:S(2)}) collective-permute-start(f32[8,16,128]{2,1,0:T(8,128)S(1)} %fusion.107), channel_id=1, source_target_pairs={{0,2},{2,4},{4,6},{6,8},{8,10},{10,12},{12,14},{14,16},{16,18},{18... | collective-permute-start | bytes 196616 | tf_op jit(solution)/shard_map/ppermute | solution.py:17
  28.7 49.3 %all-to-all-start = ((f32[128,1,16,128]{3,2,1,0:T(8,128)}), f32[128,1,16,128]{3,2,1,0:T(8,128)}, u32[]{:S(2)}, u32[]{:S(2)}) async-start(f32[128,1,16,128]{3,2,1,0:T(8,128)} %stack.2), calls=%async_computation.2 | async-start | bytes 2097152 | tf_op jit(solution)/shard_map/all_to_all | solution.py:62
  49.4 83.7 %reduce-scatter.6.cloned.1.call-start = ((), (), s32[]{:S(2)}) async-start(), calls=%async_computation.5 | async-start | bytes 24576 | tf_op jit(solution)/shard_map/reduce_scatter | solution.py:33
  60.5 11.0 %collective-permute-start.3 = (f32[8,16,128]{2,1,0:T(8,128)S(1)}, f32[8,16,128]{2,1,0:T(8,128)S(1)}, u32[]{:S(2)}, u32[]{:S(2)}) collective-permute-start(f32[8,16,128]{2,1,0:T(8,128)S(1)} %fusion.107), channel_id=1, source_target_pairs={{2,0},{4,2},{6,4},{8,6},{10,8},{12,10},{14,12},{16,14},{18,16},{20... | collective-permute-start | bytes 196616 | tf_op jit(solution)/shard_map/ppermute | solution.py:18
  67.0 66.1 %reduce-scatter.8.cloned.1.call-start = ((), (), s32[]{:S(2)}) async-start(), calls=%async_computation.6 | async-start | bytes 24576 | tf_op jit(solution)/shard_map/reduce_scatter | solution.py:33
  76.8 11.4 %copy-start.17 = (pred[8,8]{1,0:T(8,128)(4,1)S(1)}, pred[8,8]{1,0:T(8,128)(4,1)}, u32[]{:S(2)}) copy-start(pred[8,8]{1,0:T(8,128)(4,1)} %get-tuple-element.32) | copy-start | bytes 196
  88.1 46.0 %reduce-scatter.4.cloned.1.call-start = ((), (), s32[]{:S(2)}) async-start(), calls=%async_computation.4 | async-start | bytes 196608 | tf_op jit(solution)/shard_map/reduce_scatter | solution.py:33
  91.7 7.8 %copy-start.28 = (pred[8]{0:T(512)(128)(4,1)S(1)}, pred[8]{0:T(512)(128)(4,1)}, u32[]{:S(2)}) copy-start(pred[8]{0:T(512)(128)(4,1)} %get-tuple-element.44) | copy-start | bytes 28
  92.6 9.0 %copy-start.27 = (pred[8]{0:T(512)(128)(4,1)S(1)}, pred[8]{0:T(512)(128)(4,1)}, u32[]{:S(2)}) copy-start(pred[8]{0:T(512)(128)(4,1)} %get-tuple-element.43) | copy-start | bytes 28
  96.2 11.7 %copy-start.14 = (f32[1,3,8,256]{3,2,1,0:T(8,128)S(1)}, f32[1,3,8,256]{3,2,1,0:T(8,128)}, u32[]{:S(2)}) copy-start(f32[1,3,8,256]{3,2,1,0:T(8,128)} %copy.96) | copy-start | bytes 73732
  107.9 11.0 %copy-start.26 = (f32[8]{0:T(128)S(1)}, f32[8]{0:T(128)}, u32[]{:S(2)}) copy-start(f32[8]{0:T(128)} %get-tuple-element.20) | copy-start | bytes 100
  130.5 6.2 %copy-start.32 = (f32[8]{0:T(128)S(1)}, f32[8]{0:T(128)}, u32[]{:S(2)}) copy-start(f32[8]{0:T(128)} %get-tuple-element.14) | copy-start | bytes 100
  (20 other events, 62.9 us)
Sparse Core Ops, SparseCore 0:
  67.1 15.3 reduce-scatter.5
  88.2 10.7 reduce-scatter.7
  101.5 14.1 reduce-scatter.3
